TPU v7x, 32 devices: a whole 2x2x4 slice. The times are simulated.
32 devices in a mesh: seq: 8 (over z, y), rows: 4 (over x, core).
Axes of the slice: x: 2, y: 2, z: 4, core: 2. Of those that a mesh axis runs over, the one named last changes fastest.
Arguments:
- hidden: bfloat16 [4, 1024, 768], P('rows', 'seq'), may hold values from -6 to 6
- cotangent: bfloat16 [4, 1024, 768], P('rows', 'seq'), may hold values from -6 to 6
- segment_ids: int32 [4, 1024], P('rows', 'seq'), may hold values from 0 to 15, never falling along the last dimension, each value on 1 to 768 neighbouring positions
- timesteps: int32 [4, 16], P('rows'), may hold values from 0 to 4999
- qkv_weight: bfloat16 [768, 2304], replicated, may hold values from -0.21875 to 0.21875
- qv_bias: float32 [1536], replicated, may hold values from -3 to 3
- out_weight: bfloat16 [768, 768], replicated, may hold values from -1.75 to 1.75
- out_bias: float32 [768], replicated, may hold values from -3 to 3
- up_weight: bfloat16 [768, 3072], replicated, may hold values from -0.21875 to 0.21875
- up_bias: float32 [3072], replicated, may hold values from -3 to 3
- down_weight: bfloat16 [3072, 768], replicated, may hold values from -0.109375 to 0.109375
- down_bias: float32 [768], replicated, may hold values from -3 to 3
- norm_gain: float32 [2, 768], replicated, may hold values from 0.1 to 1.9
- norm_bias: float32 [2, 768], replicated, may hold values from -3 to 3
- time_weight: bfloat16 [768, 768], replicated, may hold values from -0.21875 to 0.21875
Outputs:
- result: bfloat16 [4, 1024, 768], P('rows', 'seq')
- input_grad: float32 [4, 1024, 768], P('rows', 'seq')
- grad_qkv_weight: float32 [768, 2304], P('seq')
- grad_qv_bias: float32 [1536], P('seq')
- grad_out_weight: float32 [768, 768], P('seq')
- grad_out_bias: float32 [768], P('seq')
- grad_up_weight: float32 [768, 3072], P('seq')
- grad_up_bias: float32 [3072], P('seq')
- grad_down_weight: float32 [3072, 768], P('seq')
- grad_down_bias: float32 [768], P('seq')
- grad_norm_gain: float32 [2, 768], P(None, 'seq')
- grad_norm_bias: float32 [2, 768], P(None, 'seq')
- grad_time_weight: float32 [768, 768], P('seq')
Inputs may be any that keep to these rules, and one draw needn't show every extreme that they name: `segment_ids`: along each row the ids never fall; each of the 16 documents covers 1 to 768 consecutive tokens, and one of each row covers exactly 768.
All inputs are finite; a program needn't handle non-finite values.
Results may differ from a plain program's by a relative error of at most 0.023.
Values may be sent and summed in bfloat16 or wider, within the bound.
No kernel may reach another device: no remote copies, remote signals or barrier semaphores. Data moves between devices by JAX's collectives and lax.ppermute only.
A program may use at most 192 MiB of HBM per device.

v0:
```python
import math
import jax
import jax.numpy as jnp
from jax import lax
from jax.sharding import PartitionSpec as P

D = 768
H = 12
HD = 64
DOCS = 16
EPS = 1e-05
NEG_BIG = -1e30
precise = lax.Precision.HIGHEST


def shifted(block, axis, distance):
    devices = range(lax.axis_size(axis))
    route = [((i - distance) % len(devices), i) for i in devices]
    return lax.ppermute(block, axis, route)


def time_features(timesteps):
    half_width = D // 2
    frequency = jnp.exp(
        jnp.arange(half_width, dtype=jnp.float32) * (-math.log(10000.0) / half_width)
    )
    phases = timesteps.astype(jnp.float32)[..., None] * frequency
    return jnp.concatenate([jnp.sin(phases), jnp.cos(phases)], axis=-1)


def layer_norm(residual, gain_row, offset):
    average = jnp.mean(residual, axis=-1, keepdims=True)
    centered = residual - average
    inverse = lax.rsqrt(jnp.mean(centered * centered, axis=-1, keepdims=True) + EPS)
    return centered * inverse * gain_row + offset


def gelu_exact(values):
    return jax.nn.gelu(values, approximate=False)


def divisor_under(total, limit):
    chosen = 1
    for candidate in range(1, min(total, limit) + 1):
        if total % candidate == 0:
            chosen = candidate
    return chosen


def body(
    hidden,
    cotangent,
    segment_ids,
    timesteps,
    qkv_weight,
    qv_bias,
    out_weight,
    out_bias,
    up_weight,
    up_bias,
    down_weight,
    down_bias,
    norm_gain,
    norm_bias,
    time_weight,
):
    row_count = hidden.shape[0]
    seq_rows = hidden.shape[1]
    tokens = row_count * seq_rows
    score_scale = HD ** (-0.5)
    all_docs = lax.all_gather(segment_ids, "seq", axis=1, tiled=True)
    features = time_features(timesteps).astype(jnp.bfloat16)
    doc_embed = jnp.einsum("rkd,de->rke", features, time_weight, preferred_element_type=jnp.float32)
    onehot = (segment_ids[..., None] == jnp.arange(DOCS, dtype=jnp.int32)).astype(jnp.float32)
    embedded = jnp.einsum("rsk,rke->rse", onehot, doc_embed, precision=precise)
    inputs = (hidden.astype(jnp.float32) + embedded).reshape(tokens, D)
    inputs_low = inputs.astype(jnp.bfloat16)
    projected = jnp.dot(inputs_low, qkv_weight, preferred_element_type=jnp.float32)
    queries = (projected[:, :D] + qv_bias[:D]).astype(jnp.bfloat16)
    keys_own = projected[:, D : 2 * D].astype(jnp.bfloat16).reshape(row_count, seq_rows, D)
    values_own = (
        (projected[:, 2 * D :] + qv_bias[D:]).astype(jnp.bfloat16).reshape(row_count, seq_rows, D)
    )
    query_heads = queries.reshape(row_count, seq_rows, H, HD)
    initial = (
        jnp.full((row_count, H, seq_rows), NEG_BIG, jnp.float32),
        jnp.zeros((row_count, H, seq_rows), jnp.float32),
        jnp.zeros((row_count, H, seq_rows, HD), jnp.float32),
    )
    fold_state = initial
    key_piece = lax.all_gather(keys_own, "seq", axis=1, tiled=True)
    value_piece = lax.all_gather(values_own, "seq", axis=1, tiled=True)
    width_keys = key_piece.shape[1]
    block_rows = divisor_under(width_keys, 1024)
    block_count = width_keys // block_rows
    key_blocks = jnp.moveaxis(key_piece.reshape(row_count, block_count, block_rows, H, HD), 1, 0)
    value_blocks = jnp.moveaxis(
        value_piece.reshape(row_count, block_count, block_rows, H, HD), 1, 0
    )
    doc_blocks = jnp.moveaxis(all_docs.reshape(row_count, block_count, block_rows), 1, 0)

    def absorb(run_state, block_item):
        run_max, run_sum, run_acc = run_state
        key_block, value_block, doc_block = block_item
        scores = (
            jnp.einsum(
                "rqhd,rkhd->rhqk", query_heads, key_block, preferred_element_type=jnp.float32
            )
            * score_scale
        )
        same_doc = segment_ids[:, None, :, None] == doc_block[:, None, None, :]
        new_max = jnp.maximum(run_max, jnp.max(jnp.where(same_doc, scores, NEG_BIG), axis=-1))
        weights = jnp.where(same_doc, jnp.exp(scores - new_max[..., None]), 0.0)
        factor = jnp.exp(run_max - new_max)
        run_sum = run_sum * factor + jnp.sum(weights, axis=-1)
        run_acc = run_acc * factor[..., None] + jnp.einsum(
            "rhqk,rkhd->rhqd",
            weights.astype(jnp.bfloat16),
            value_block,
            preferred_element_type=jnp.float32,
        )
        return ((new_max, run_sum, run_acc), None)

    fold_state, _ = lax.scan(absorb, fold_state, (key_blocks, value_blocks, doc_blocks))
    run_max, run_sum, run_acc = fold_state
    attended_heads = run_acc / run_sum[..., None]
    log_total = run_max + jnp.log(run_sum)
    attended = jnp.transpose(attended_heads, (0, 2, 1, 3)).reshape(tokens, D)
    attended_low = attended.astype(jnp.bfloat16)
    branch = jnp.dot(attended_low, out_weight, preferred_element_type=jnp.float32) + out_bias
    normed_one, first_pull = jax.vjp(layer_norm, inputs + branch, norm_gain[0], norm_bias[0])
    first_low = normed_one.astype(jnp.bfloat16)
    up_values = jnp.dot(first_low, up_weight, preferred_element_type=jnp.float32) + up_bias
    activated, gelu_pull = jax.vjp(gelu_exact, up_values)
    activated_low = activated.astype(jnp.bfloat16)
    ffn_out = jnp.dot(activated_low, down_weight, preferred_element_type=jnp.float32) + down_bias
    output, second_pull = jax.vjp(layer_norm, normed_one + ffn_out, norm_gain[1], norm_bias[1])
    result = output.astype(jnp.bfloat16).reshape(row_count, seq_rows, D)
    grad_second, gain_two, bias_two = second_pull(cotangent.astype(jnp.float32).reshape(tokens, D))
    down_low = grad_second.astype(jnp.bfloat16)
    grad_down_weight = jnp.einsum(
        "nf,nd->fd", activated_low, down_low, preferred_element_type=jnp.float32
    )
    grad_down_bias = jnp.sum(down_low.astype(jnp.float32), axis=0)
    activ_grad = jnp.einsum("nd,fd->nf", down_low, down_weight, preferred_element_type=jnp.float32)
    upper_low = gelu_pull(activ_grad)[0].astype(jnp.bfloat16)
    grad_up_weight = jnp.einsum(
        "nd,nf->df", first_low, upper_low, preferred_element_type=jnp.float32
    )
    grad_up_bias = jnp.sum(upper_low.astype(jnp.float32), axis=0)
    grad_first = grad_second + jnp.einsum(
        "nf,df->nd", upper_low, up_weight, preferred_element_type=jnp.float32
    )
    grad_resid, gain_one, bias_one = first_pull(grad_first)
    branch_low = grad_resid.astype(jnp.bfloat16)
    grad_out_weight = jnp.einsum(
        "nd,ne->de", attended_low, branch_low, preferred_element_type=jnp.float32
    )
    grad_out_bias = jnp.sum(branch_low.astype(jnp.float32), axis=0)
    attn_grad_low = jnp.einsum(
        "ne,de->nd", branch_low, out_weight, preferred_element_type=jnp.float32
    ).astype(jnp.bfloat16)
    grad_heads = attn_grad_low.reshape(row_count, seq_rows, H, HD)
    row_delta = jnp.einsum(
        "rqhd,rhqd->rhq", grad_heads.astype(jnp.float32), attended_heads, precision=precise
    )

    def block_grads(key_heads, value_heads, block_docs):
        width_keys = key_heads.shape[1]
        scores = (
            jnp.einsum(
                "rqhd,rkhd->rhqk", query_heads, key_heads, preferred_element_type=jnp.float32
            )
            * score_scale
        )
        same_doc = segment_ids[:, None, :, None] == block_docs[:, None, None, :]
        probabilities = jnp.where(same_doc, jnp.exp(scores - log_total[..., None]), 0.0)
        probs_low = probabilities.astype(jnp.bfloat16)
        value_part = jnp.einsum(
            "rhqk,rqhd->rkhd", probs_low, grad_heads, preferred_element_type=jnp.float32
        ).reshape(row_count, width_keys, D)
        prob_grad = jnp.einsum(
            "rqhd,rkhd->rhqk", grad_heads, value_heads, preferred_element_type=jnp.float32
        )
        score_low = (probabilities * (prob_grad - row_delta[..., None])).astype(jnp.bfloat16)
        query_part = (
            jnp.einsum("rhqk,rkhd->rqhd", score_low, key_heads, preferred_element_type=jnp.float32)
            * score_scale
        )
        key_part = (
            jnp.einsum(
                "rhqk,rqhd->rkhd", score_low, query_heads, preferred_element_type=jnp.float32
            )
            * score_scale
        ).reshape(row_count, width_keys, D)
        return (query_part, key_part, value_part)

    my_index = lax.axis_index("seq")
    cycle_size = lax.axis_size("seq")

    def cycle_turn(turn_index, cycle_state):
        key_block, value_block, key_grad, value_grad, query_grad = cycle_state
        anchor = (my_index - turn_index + cycle_size) % cycle_size
        block_docs = lax.dynamic_slice_in_dim(all_docs, anchor * seq_rows, seq_rows, 1)
        query_part, key_part, value_part = block_grads(
            key_block.reshape(row_count, seq_rows, H, HD),
            value_block.reshape(row_count, seq_rows, H, HD),
            block_docs,
        )
        query_grad = query_grad + query_part
        key_grad = key_grad + key_part
        value_grad = value_grad + value_part
        key_block, value_block = shifted((key_block, value_block), "seq", 1)
        key_grad, value_grad = (
            shifted(key_grad.astype(jnp.bfloat16), "seq", 1).astype(key_grad.dtype),
            shifted(value_grad.astype(jnp.bfloat16), "seq", 1).astype(value_grad.dtype),
        )
        return (key_block, value_block, key_grad, value_grad, query_grad)

    cycle_init = (
        keys_own,
        values_own,
        jnp.zeros((row_count, seq_rows, D), jnp.float32),
        jnp.zeros((row_count, seq_rows, D), jnp.float32),
        jnp.zeros((row_count, seq_rows, H, HD), jnp.float32),
    )
    cycle_done = lax.fori_loop(0, cycle_size, cycle_turn, cycle_init)
    query_total, key_total, value_total = (cycle_done[4], cycle_done[2], cycle_done[3])
    query_low = query_total.reshape(tokens, D).astype(jnp.bfloat16)
    key_low = key_total.reshape(tokens, D).astype(jnp.bfloat16)
    value_low = value_total.reshape(tokens, D).astype(jnp.bfloat16)
    packed = jnp.concatenate([query_low, key_low, value_low], axis=1)
    grad_qkv_weight = jnp.einsum(
        "nd,ne->de", inputs_low, packed, preferred_element_type=jnp.float32
    )
    grad_qv_bias = jnp.concatenate(
        [
            jnp.sum(query_low.astype(jnp.float32), axis=0),
            jnp.sum(value_low.astype(jnp.float32), axis=0),
        ]
    )
    input_grad = grad_resid + jnp.einsum(
        "ne,de->nd", packed, qkv_weight, preferred_element_type=jnp.float32
    )
    input_grad = input_grad.reshape(row_count, seq_rows, D)
    doc_grad = jnp.einsum("rsk,rsd->rkd", onehot, input_grad, precision=precise)
    grad_time_weight = jnp.einsum(
        "rkd,rke->de", features.astype(jnp.float32), doc_grad, precision=precise
    )
    grad_norm_gain = jnp.stack([gain_one, gain_two])
    grad_norm_bias = jnp.stack([bias_one, bias_two])
    local_grads = (
        grad_qkv_weight,
        grad_qv_bias,
        grad_out_weight,
        grad_out_bias,
        grad_up_weight,
        grad_up_bias,
        grad_down_weight,
        grad_down_bias,
        grad_norm_gain,
        grad_norm_bias,
        grad_time_weight,
    )
    stacked_flags = (False, False, False, False, False, False, False, False, True, True, False)
    seq_count = lax.axis_size("seq")
    laid_out = []
    for grad_piece, stacked in zip(local_grads, stacked_flags):
        if stacked:
            laid_out.append(
                jnp.transpose(grad_piece.reshape(2, seq_count, -1), (1, 0, 2)).reshape(
                    seq_count, -1
                )
            )
        else:
            laid_out.append(grad_piece.reshape(seq_count, -1))
    flat_grads = jnp.concatenate(laid_out, axis=1)
    share_width = flat_grads.shape[1]
    row_count_axis = lax.axis_size("rows")
    padding = -share_width % row_count_axis
    split_rows = flat_grads.reshape(
        seq_count * row_count_axis, (share_width + padding) // row_count_axis
    )
    shares = lax.psum_scatter(split_rows, ("seq", "rows"), scatter_dimension=0, tiled=True)
    whole = lax.all_gather(shares.astype(jnp.bfloat16), "rows", axis=0, tiled=True).astype(
        shares.dtype
    )
    mine = whole.reshape(-1)
    outputs_list = [result, input_grad]
    position = 0
    for grad_piece, stacked in zip(local_grads, stacked_flags):
        count = grad_piece.size // seq_count
        segment = mine[position : position + count]
        if stacked:
            outputs_list.append(segment.reshape(2, grad_piece.shape[1] // seq_count))
        else:
            outputs_list.append(
                segment.reshape((grad_piece.shape[0] // seq_count,) + grad_piece.shape[1:])
            )
        position += count
    return tuple(outputs_list)


def solution(mesh):
    return jax.shard_map(
        body,
        mesh=mesh,
        in_specs=(
            P("rows", "seq", None),
            P("rows", "seq", None),
            P("rows", "seq"),
            P("rows", None),
            P(),
            P(),
            P(),
            P(),
            P(),
            P(),
            P(),
            P(),
            P(),
            P(),
            P(),
        ),
        out_specs=(
            P("rows", "seq", None),
            P("rows", "seq", None),
            P("seq", None),
            P("seq"),
            P("seq", None),
            P("seq"),
            P("seq", None),
            P("seq"),
            P("seq", None),
            P("seq"),
            P(None, "seq"),
            P(None, "seq"),
            P("seq", None),
        ),
        check_vma=False,
    )
```

profile of v0, /device:TPU:0, one launch (start us, length us, event | category | flops | bytes accessed | tf_op | source)
XLA Modules:
  0.0 1149.3 jit_solution(14988583280119527673)
XLA Ops:
  13.7 1.9 fusion.44
  24.3 22.2 %all_gather.14 = s32[1,1024]{1,0:T(1,128)S(1)} all-gather(s32[1,128]{1,0:T(1,128)S(1)} %copy-done.36), channel_id=1, replica_groups=mesh['seq'=8,'rows'=4] {'seq'}, dimensions={1}, use_global_device_ids=true | all-gather | bytes 4608 | tf_op jit(solution)/shard_map/all_gather | solution.py:71
  48.8 11.9 %all-gather.7.cloned.1.call-done = bf16[1024,768]{1,0:T(8,128)(2,1)} async-done(((bf16[128,768]{1,0:T(8,128)(2,1)}), bf16[1024,768]{1,0:T(8,128)(2,1)}) %all-gather.7.cloned.1.call-update) | async-done | bytes 1572880 | tf_op jit(solution)/shard_map/all_gather | solution.py:91
  60.7 2.6 copy.44
  63.3 2.7 select_reduce_fusion
  66.1 1.8 fusion.15
  69.9 36.6 %all-gather.9.cloned.1.call-done = bf16[1024,768]{1,0:T(8,128)(2,1)} async-done(((bf16[128,768]{1,0:T(8,128)(2,1)}), bf16[1024,768]{1,0:T(8,128)(2,1)}) %all-gather.9.cloned.1.call-update) | async-done | bytes 1572880 | tf_op jit(solution)/shard_map/all_gather | solution.py:92
  106.5 2.8 copy.45
  109.3 5.7 fusion.83
  115.9 4.2 multiply_convert_fusion
  123.6 2.4 convert_reduce_fusion.1
  126.0 2.4 multiply_reduce_fusion
  134.9 193.8 %while.30 = (s32[]{:T(128)}, bf16[1,128,768]{1,2,0:T(8,128)(2,1)}, bf16[1,128,768]{1,2,0:T(8,128)(2,1)}, f32[1,128,768]{1,2,0:T(8,128)}, f32[1,128,768]{1,2,0:T(...) while((s32[]{:T(128)}, bf16[1,128,768]{1,2,0:T(8,128)(2,1)}, ...), condition=%wide.region_11.12_spmd.clone, body=%wide.region_10.11_spmd.clone.sunk | while | flops 128401424 | bytes 19905180 | solution.py:227
  138.9 2.8 collective-permute-start.1
  150.4 2.2 fusion.149
  152.6 5.1 collective-permute-done.2
  171.9 2.5 collective-permute-start.3
  174.4 2.3 fusion.149
  176.7 4.4 collective-permute-done.2
  194.9 2.5 collective-permute-start.3
  197.4 2.3 fusion.149
  199.7 4.6 collective-permute-done.2
  219.2 2.0 collective-permute-start.3
  221.2 2.3 fusion.149
  223.5 4.2 collective-permute-done.2
  242.3 2.0 collective-permute-start.3
  244.3 2.3 fusion.149
  246.7 4.4 collective-permute-done.2
  265.6 2.1 collective-permute-start.3
  267.7 2.3 fusion.149
  270.0 4.8 collective-permute-done.2
  289.4 2.1 collective-permute-start.3
  291.5 2.3 fusion.149
  293.8 5.6 collective-permute-done.2
  313.7 1.9 collective-permute-start.3
  315.6 2.3 fusion.149
  317.9 6.1 collective-permute-done.2
  332.7 2.1 convolution_add_fusion.2
  334.8 4.0 fusion.47
  338.9 1.9 fusion.86
  340.8 5.0 fusion.72
  345.8 5.0 fusion.87
  350.8 7.1 reshape.640
  357.9 5.5 constant_dynamic-update-slice_fusion.1
  363.6 2.1 reshape.641
  365.8 8.9 reshape.643
  374.8 8.9 reshape.645
  384.6 2.6 fusion.57
  387.2 3.5 reshape.649
  392.0 7.5 dynamic-update-slice.2
  401.0 26.5 %dynamic-update-slice.4 = f32[8,959616]{1,0:T(8,128)} dynamic-update-slice(f32[8,959616]{1,0:T(8,128)} %dynamic-update-slice.3, f32[8,294912]{1,0:T(8,128)} %reshape.643, s32[]{} %constant.210, s32[]{} %constant.215) | dynamic-update-slice | bytes 18874372
  428.9 26.6 %dynamic-update-slice.6 = f32[8,959616]{1,0:T(8,128)} dynamic-update-slice(f32[8,959616]{1,0:T(8,128)} %dynamic-update-slice.5, f32[8,294912]{1,0:T(8,128)} %reshape.645, s32[]{} %constant.210, s32[]{} %constant.217) | dynamic-update-slice | bytes 18874372
  461.5 37.1 %reshape.681 = f32[7676928]{0:T(1024)} reshape(f32[8,959616]{1,0:T(8,128)} %constant_dynamic-update-slice_fusion) | data formatting | bytes 61415424
  498.6 41.0 %reshape.650 = f32[32,239904]{1,0:T(8,128)} reshape(f32[7676928]{0:T(1024)} %reshape.681) | data formatting | bytes 61415424 | tf_op jit(solution)/shard_map/reshape | solution.py:281
  539.6 492.5 %all-reduce.2 = bf16[32,239904]{1,0:T(8,128)(2,1)} all-reduce(f32[32,239904]{1,0:T(8,128)} %reshape.650), channel_id=4, replica_groups=mesh['seq'=8,'rows'=4] {'seq','rows'}, use_global_device_ids=true, to_apply=%region_21.22.clone | all-reduce | flops 7676928 | bytes 46061568
  1032.1 3.4 fusion.36
  1035.5 29.7 %all-gather.11.cloned.1.call-done = bf16[4,1,239904]{2,1,0:T(2,128)(2,1)} async-done(((bf16[1,1,239904]{2,1,0:T(2,128)(2,1)}), bf16[4,1,239904]{2,1,0:T(2,128)(2,1)}) %all-gather.11.cloned.1.call-update) | async-done | bytes 1919248 | tf_op jit(solution)/shard_map/all_gather | solution.py:285
  1065.2 43.7 %convert_reduce_fusion = f32[4,239904]{1,0:T(4,128)} fusion(bf16[4,1,239904]{2,1,0:T(2,128)(2,1)} %all-gather.11.cloned.1.call-done), kind=kLoop, calls=%fused_computation.27 | loop fusion | flops 959616 | bytes 5757696 | tf_op jit(solution)/shard_map/convert_element_type | solution.py:285
  1108.8 6.5 reshape.651
  1116.6 1.9 fusion.79
  1119.7 3.9 fusion.81
  1124.2 8.4 slice.82
  1134.5 2.6 reshape.654
  1137.0 2.4 reshape.655
  (423 shorter events, 170.6 us)
Async XLA Ops:
  7.2 53.5 %all-gather.7.cloned.1.call-start = ((), (), s32[]{:S(2)}) async-start(), calls=%async_computation | async-start | bytes 1769472 | tf_op jit(solution)/shard_map/all_gather | solution.py:91
  13.6 92.8 %all-gather.9.cloned.1.call-start = ((), (), s32[]{:S(2)}) async-start(), calls=%async_computation.1 | async-start | bytes 1769472 | tf_op jit(solution)/shard_map/all_gather | solution.py:92
  13.7 10.6 copy-start.36
  15.7 1049.5 %all-gather.11.cloned.1.call-start = ((), (), s32[]{:S(2)}) async-start(), calls=%async_computation.2 | async-start | bytes 4800000 | tf_op jit(solution)/shard_map/all_gather | solution.py:285
  109.3 6.5 slice-start.3
  109.3 5.8 copy-start.13
  109.3 5.7 copy-start.16
  109.3 5.7 copy-start.54
  109.3 6.5 slice-start.4
  115.1 5.0 slice-start.1
  115.5 12.9 %copy-start.5 = (f32[128,768]{1,0:T(8,128)}, f32[128,768]{1,0:T(8,128)S(1)}, u32[]{:S(2)}) copy-start(f32[128,768]{1,0:T(8,128)S(1)} %get-tuple-element.508) | copy-start | bytes 1179652
  115.6 12.9 %copy-start.39 = (f32[128]{0:T(128)}, f32[128]{0:T(128)S(1)}, u32[]{:S(2)}) copy-start(f32[128]{0:T(128)S(1)} %broadcast_multiply_fusion.1) | copy-start | bytes 1540
  115.8 12.7 %copy-start.50 = (f32[128]{0:T(128)}, f32[128]{0:T(128)S(1)}, u32[]{:S(2)}) copy-start(f32[128]{0:T(128)S(1)} %fusion.63) | copy-start | bytes 1540
  136.7 24.8 %collective-permute-start = (bf16[1,128,768]{1,2,0:T(8,128)(2,1)}, bf16[1,128,768]{1,2,0:T(8,128)(2,1)}, u32[]{:S(2)}, u32[]{:S(2)}) collective-permute-start(bf16[1,128,768]{1,2,0:T(8,128)(2,1)} %copy.66), channel_id=1, source_target_pairs={{28,0},{0,4},{4,8},{8,12},{12,16},{16,20},{20,24},{24,28},{29,1},{... | collective-permute-start | bytes 589832 | tf_op jit(solution)/shard_map/while/body/eval_jaxpr/ppermute | solution.py:19
  138.9 22.6 %collective-permute-start.1 = (bf16[1,128,768]{1,2,0:T(8,128)(2,1)}, bf16[1,128,768]{1,2,0:T(8,128)(2,1)}, u32[]{:S(2)}, u32[]{:S(2)}) collective-permute-start(bf16[1,128,768]{1,2,0:T(8,128)(2,1)} %copy.67), channel_id=1, source_target_pairs={{28,0},{0,4},{4,8},{8,12},{12,16},{16,20},{20,24},{24,28},{29,1},{... | collective-permute-start | bytes 589832 | tf_op jit(solution)/shard_map/while/body/eval_jaxpr/ppermute | solution.py:19
  147.1 10.5 collective-permute-start.2
  148.7 11.1 collective-permute-start.3
  163.1 21.9 %collective-permute-start = (bf16[1,128,768]{1,2,0:T(8,128)(2,1)}, bf16[1,128,768]{1,2,0:T(8,128)(2,1)}, u32[]{:S(2)}, u32[]{:S(2)}) collective-permute-start(bf16[1,128,768]{1,2,0:T(8,128)(2,1)} %copy.66), channel_id=1, source_target_pairs={{28,0},{0,4},{4,8},{8,12},{12,16},{16,20},{20,24},{24,28},{29,1},{... | collective-permute-start | bytes 589832 | tf_op jit(solution)/shard_map/while/body/eval_jaxpr/ppermute | solution.py:19
  164.8 20.2 %collective-permute-start.1 = (bf16[1,128,768]{1,2,0:T(8,128)(2,1)}, bf16[1,128,768]{1,2,0:T(8,128)(2,1)}, u32[]{:S(2)}, u32[]{:S(2)}) collective-permute-start(bf16[1,128,768]{1,2,0:T(8,128)(2,1)} %copy.67), channel_id=1, source_target_pairs={{28,0},{0,4},{4,8},{8,12},{12,16},{16,20},{20,24},{24,28},{29,1},{... | collective-permute-start | bytes 589832 | tf_op jit(solution)/shard_map/while/body/eval_jaxpr/ppermute | solution.py:19
  170.9 10.2 collective-permute-start.2
  171.9 11.3 collective-permute-start.3
  186.6 21.5 %collective-permute-start = (bf16[1,128,768]{1,2,0:T(8,128)(2,1)}, bf16[1,128,768]{1,2,0:T(8,128)(2,1)}, u32[]{:S(2)}, u32[]{:S(2)}) collective-permute-start(bf16[1,128,768]{1,2,0:T(8,128)(2,1)} %copy.66), channel_id=1, source_target_pairs={{28,0},{0,4},{4,8},{8,12},{12,16},{16,20},{20,24},{24,28},{29,1},{... | collective-permute-start | bytes 589832 | tf_op jit(solution)/shard_map/while/body/eval_jaxpr/ppermute | solution.py:19
  188.2 19.9 %collective-permute-start.1 = (bf16[1,128,768]{1,2,0:T(8,128)(2,1)}, bf16[1,128,768]{1,2,0:T(8,128)(2,1)}, u32[]{:S(2)}, u32[]{:S(2)}) collective-permute-start(bf16[1,128,768]{1,2,0:T(8,128)(2,1)} %copy.67), channel_id=1, source_target_pairs={{28,0},{0,4},{4,8},{8,12},{12,16},{16,20},{20,24},{24,28},{29,1},{... | collective-permute-start | bytes 589832 | tf_op jit(solution)/shard_map/while/body/eval_jaxpr/ppermute | solution.py:19
  188.4 4.4 copy-start.10
  193.9 10.4 collective-permute-start.2
  194.9 11.6 %collective-permute-start.3 = (bf16[1,128,768]{1,2,0:T(8,128)(2,1)}, bf16[1,128,768]{1,2,0:T(8,128)(2,1)}, u32[]{:S(2)}, u32[]{:S(2)}) collective-permute-start(bf16[1,128,768]{1,2,0:T(8,128)(2,1)} %fusion.148), channel_id=1, source_target_pairs={{28,0},{0,4},{4,8},{8,12},{12,16},{16,20},{20,24},{24,28},{29,1},{... | collective-permute-start | bytes 589832 | tf_op jit(solution)/shard_map/while/body/eval_jaxpr/ppermute | solution.py:19
  209.8 21.8 %collective-permute-start = (bf16[1,128,768]{1,2,0:T(8,128)(2,1)}, bf16[1,128,768]{1,2,0:T(8,128)(2,1)}, u32[]{:S(2)}, u32[]{:S(2)}) collective-permute-start(bf16[1,128,768]{1,2,0:T(8,128)(2,1)} %copy.66), channel_id=1, source_target_pairs={{28,0},{0,4},{4,8},{8,12},{12,16},{16,20},{20,24},{24,28},{29,1},{... | collective-permute-start | bytes 589832 | tf_op jit(solution)/shard_map/while/body/eval_jaxpr/ppermute | solution.py:19
  211.4 20.1 %collective-permute-start.1 = (bf16[1,128,768]{1,2,0:T(8,128)(2,1)}, bf16[1,128,768]{1,2,0:T(8,128)(2,1)}, u32[]{:S(2)}, u32[]{:S(2)}) collective-permute-start(bf16[1,128,768]{1,2,0:T(8,128)(2,1)} %copy.67), channel_id=1, source_target_pairs={{28,0},{0,4},{4,8},{8,12},{12,16},{16,20},{20,24},{24,28},{29,1},{... | collective-permute-start | bytes 589832 | tf_op jit(solution)/shard_map/while/body/eval_jaxpr/ppermute | solution.py:19
  211.4 4.5 copy-start.10
  216.9 10.8 collective-permute-start.2
  219.2 10.6 collective-permute-start.3
  233.1 22.1 %collective-permute-start = (bf16[1,128,768]{1,2,0:T(8,128)(2,1)}, bf16[1,128,768]{1,2,0:T(8,128)(2,1)}, u32[]{:S(2)}, u32[]{:S(2)}) collective-permute-start(bf16[1,128,768]{1,2,0:T(8,128)(2,1)} %copy.66), channel_id=1, source_target_pairs={{28,0},{0,4},{4,8},{8,12},{12,16},{16,20},{20,24},{24,28},{29,1},{... | collective-permute-start | bytes 589832 | tf_op jit(solution)/shard_map/while/body/eval_jaxpr/ppermute | solution.py:19
  234.8 20.5 %collective-permute-start.1 = (bf16[1,128,768]{1,2,0:T(8,128)(2,1)}, bf16[1,128,768]{1,2,0:T(8,128)(2,1)}, u32[]{:S(2)}, u32[]{:S(2)}) collective-permute-start(bf16[1,128,768]{1,2,0:T(8,128)(2,1)} %copy.67), channel_id=1, source_target_pairs={{28,0},{0,4},{4,8},{8,12},{12,16},{16,20},{20,24},{24,28},{29,1},{... | collective-permute-start | bytes 589832 | tf_op jit(solution)/shard_map/while/body/eval_jaxpr/ppermute | solution.py:19
  234.8 4.4 copy-start.10
  240.2 10.9 collective-permute-start.2
  242.3 11.2 collective-permute-start.3
  256.9 22.5 %collective-permute-start = (bf16[1,128,768]{1,2,0:T(8,128)(2,1)}, bf16[1,128,768]{1,2,0:T(8,128)(2,1)}, u32[]{:S(2)}, u32[]{:S(2)}) collective-permute-start(bf16[1,128,768]{1,2,0:T(8,128)(2,1)} %copy.66), channel_id=1, source_target_pairs={{28,0},{0,4},{4,8},{8,12},{12,16},{16,20},{20,24},{24,28},{29,1},{... | collective-permute-start | bytes 589832 | tf_op jit(solution)/shard_map/while/body/eval_jaxpr/ppermute | solution.py:19
  258.5 20.9 %collective-permute-start.1 = (bf16[1,128,768]{1,2,0:T(8,128)(2,1)}, bf16[1,128,768]{1,2,0:T(8,128)(2,1)}, u32[]{:S(2)}, u32[]{:S(2)}) collective-permute-start(bf16[1,128,768]{1,2,0:T(8,128)(2,1)} %copy.67), channel_id=1, source_target_pairs={{28,0},{0,4},{4,8},{8,12},{12,16},{16,20},{20,24},{24,28},{29,1},{... | collective-permute-start | bytes 589832 | tf_op jit(solution)/shard_map/while/body/eval_jaxpr/ppermute | solution.py:19
  264.0 10.9 collective-permute-start.2
  265.6 12.1 %collective-permute-start.3 = (bf16[1,128,768]{1,2,0:T(8,128)(2,1)}, bf16[1,128,768]{1,2,0:T(8,128)(2,1)}, u32[]{:S(2)}, u32[]{:S(2)}) collective-permute-start(bf16[1,128,768]{1,2,0:T(8,128)(2,1)} %fusion.148), channel_id=1, source_target_pairs={{28,0},{0,4},{4,8},{8,12},{12,16},{16,20},{20,24},{24,28},{29,1},{... | collective-permute-start | bytes 589832 | tf_op jit(solution)/shard_map/while/body/eval_jaxpr/ppermute | solution.py:19
  281.1 23.0 %collective-permute-start = (bf16[1,128,768]{1,2,0:T(8,128)(2,1)}, bf16[1,128,768]{1,2,0:T(8,128)(2,1)}, u32[]{:S(2)}, u32[]{:S(2)}) collective-permute-start(bf16[1,128,768]{1,2,0:T(8,128)(2,1)} %copy.66), channel_id=1, source_target_pairs={{28,0},{0,4},{4,8},{8,12},{12,16},{16,20},{20,24},{24,28},{29,1},{... | collective-permute-start | bytes 589832 | tf_op jit(solution)/shard_map/while/body/eval_jaxpr/ppermute | solution.py:19
  282.7 21.4 %collective-permute-start.1 = (bf16[1,128,768]{1,2,0:T(8,128)(2,1)}, bf16[1,128,768]{1,2,0:T(8,128)(2,1)}, u32[]{:S(2)}, u32[]{:S(2)}) collective-permute-start(bf16[1,128,768]{1,2,0:T(8,128)(2,1)} %copy.67), channel_id=1, source_target_pairs={{28,0},{0,4},{4,8},{8,12},{12,16},{16,20},{20,24},{24,28},{29,1},{... | collective-permute-start | bytes 589832 | tf_op jit(solution)/shard_map/while/body/eval_jaxpr/ppermute | solution.py:19
  288.1 11.3 collective-permute-start.2
  289.4 13.0 %collective-permute-start.3 = (bf16[1,128,768]{1,2,0:T(8,128)(2,1)}, bf16[1,128,768]{1,2,0:T(8,128)(2,1)}, u32[]{:S(2)}, u32[]{:S(2)}) collective-permute-start(bf16[1,128,768]{1,2,0:T(8,128)(2,1)} %fusion.148), channel_id=1, source_target_pairs={{28,0},{0,4},{4,8},{8,12},{12,16},{16,20},{20,24},{24,28},{29,1},{... | collective-permute-start | bytes 589832 | tf_op jit(solution)/shard_map/while/body/eval_jaxpr/ppermute | solution.py:19
  305.7 23.0 %collective-permute-start = (bf16[1,128,768]{1,2,0:T(8,128)(2,1)}, bf16[1,128,768]{1,2,0:T(8,128)(2,1)}, u32[]{:S(2)}, u32[]{:S(2)}) collective-permute-start(bf16[1,128,768]{1,2,0:T(8,128)(2,1)} %copy.66), channel_id=1, source_target_pairs={{28,0},{0,4},{4,8},{8,12},{12,16},{16,20},{20,24},{24,28},{29,1},{... | collective-permute-start | bytes 589832 | tf_op jit(solution)/shard_map/while/body/eval_jaxpr/ppermute | solution.py:19
  307.3 21.4 %collective-permute-start.1 = (bf16[1,128,768]{1,2,0:T(8,128)(2,1)}, bf16[1,128,768]{1,2,0:T(8,128)(2,1)}, u32[]{:S(2)}, u32[]{:S(2)}) collective-permute-start(bf16[1,128,768]{1,2,0:T(8,128)(2,1)} %copy.67), channel_id=1, source_target_pairs={{28,0},{0,4},{4,8},{8,12},{12,16},{16,20},{20,24},{24,28},{29,1},{... | collective-permute-start | bytes 589832 | tf_op jit(solution)/shard_map/while/body/eval_jaxpr/ppermute | solution.py:19
  312.7 11.3 collective-permute-start.2
  313.7 13.2 %collective-permute-start.3 = (bf16[1,128,768]{1,2,0:T(8,128)(2,1)}, bf16[1,128,768]{1,2,0:T(8,128)(2,1)}, u32[]{:S(2)}, u32[]{:S(2)}) collective-permute-start(bf16[1,128,768]{1,2,0:T(8,128)(2,1)} %fusion.148), channel_id=1, source_target_pairs={{28,0},{0,4},{4,8},{8,12},{12,16},{16,20},{20,24},{24,28},{29,1},{... | collective-permute-start | bytes 589832 | tf_op jit(solution)/shard_map/while/body/eval_jaxpr/ppermute | solution.py:19
  340.7 5.1 copy-start.18
  340.8 5.1 copy-start.30
  357.9 5.5 copy-start.45
  365.8 8.9 copy-start.52
  374.7 9.0 copy-start.43
  374.7 9.1 copy-start.42
  374.7 9.2 copy-start.49
  374.7 9.3 copy-start.48
  374.7 9.4 copy-start.47
  374.7 9.5 copy-start.31
  374.8 9.5 copy-start.37
  374.8 9.8 copy-start.33
  374.8 9.8 copy-start.35
  428.9 31.0 %copy-start.11 = (f32[8,73728]{1,0:T(8,128)S(1)}, f32[8,73728]{1,0:T(8,128)}, u32[]{:S(2)}) copy-start(f32[8,73728]{1,0:T(8,128)} %reshape.649) | copy-start | bytes 7077892
  1124.2 8.4 slice-start
  1134.5 8.1 copy-start.1
  (70 other events, 162.8 us)
Sparse Core Ops, SparseCore 0:
  13.8 46.8 all-gather.6
  63.4 42.9 all-gather.8
  1035.6 29.5 all-gather.10
where the time goes:
time: 1160 us; the launch traced here: 1150 us
  blocking collectives  515 us (44%)
  local copies, waits for them, and re-layouts  275 us (24%)
  waiting for transfers between devices  124 us (11%)
  other arithmetic  105 us (9%)
  matrix products  90.3 us (8%)
  starting transfers between devices  25.1 us (2%)
  between operations  14.7 us (1%)
    unnamed x1, blocking collectives  492 us
    unnamed x130, local copies, waits for them, and re-layouts  122 us
    ppermute x32, waiting for transfers between devices, shifted(): return lax.ppermute(block, axis, route)  45.3 us
    convert_element_type x1, other arithmetic, body(): lax.all_gather(shares.astype(jnp.bfloat16), 'rows', axis=0, tiled=True)  43.7 us
    reshape x1, local copies, waits for them, and re-layouts, body(): flat_grads.reshape(seq_count * row_count_axis, (share_width + padding) //...  41 us
    all_gather x1, waiting for transfers between devices, body(): value_piece = lax.all_gather(values_own, 'seq', axis=1, tiled=True)  36.6 us
    reshape x8, local copies, waits for them, and re-layouts, body(): laid_out.append(grad_piece.reshape(seq_count, -1))  30.7 us
    all_gather x1, waiting for transfers between devices, body(): lax.all_gather(shares.astype(jnp.bfloat16), 'rows', axis=0, tiled=True)  29.7 us
  transfers between devices with their start and end apart: 35, of which 19 were waited for; matrix products, arithmetic and copies ran while one was open for 11% of the time, Pallas kernels for 0%

commit v1 on v0

--- a/solution.py
+++ b/solution.py
@@ -11,6 +11,24 @@
 EPS = 1e-05
 NEG_BIG = -1e30
 precise = lax.Precision.HIGHEST
+
+
+def in_order(parts, dim):
+    shape = list(parts.shape[1:])
+    shape[dim] *= parts.shape[0]
+    return jnp.moveaxis(parts, 0, dim).reshape(shape)
+
+
+def collected_by_bits(x, axis):
+    size = lax.axis_size(axis)
+    blocks = x[None]
+    for level in range(size.bit_length() - 1):
+        stride = 1 << level
+        theirs = lax.ppermute(blocks, axis, [(i, i ^ stride) for i in range(size)])
+        both = jnp.stack([blocks, theirs])
+        upper = lax.axis_index(axis) >> level & 1
+        blocks = jnp.where(upper == 0, both, both[::-1]).reshape(-1, *x.shape)
+    return blocks
 
 
 def shifted(block, axis, distance):
@@ -89,7 +107,7 @@
     )
     fold_state = initial
     key_piece = lax.all_gather(keys_own, "seq", axis=1, tiled=True)
-    value_piece = lax.all_gather(values_own, "seq", axis=1, tiled=True)
+    value_piece = in_order(collected_by_bits(values_own, "seq"), 1)
     width_keys = key_piece.shape[1]
     block_rows = divisor_under(width_keys, 1024)
     block_count = width_keys // block_rows

time: 1160 us -> 1160 us (level)
  waiting for transfers between devices: 124 us -> 83 us
  starting transfers between devices: 25.1 us -> 51.6 us
    all_gather x1 -> x0, waiting for transfers between devices: 36.6 us -> none  [body(): value_piece = lax.all_gather(values_own, 'seq', axis=1, tiled=True)]
    ppermute x0 -> x3, waiting for transfers between devices: none -> 27 us  [collected_by_bits(): theirs = lax.ppermute(blocks, axis, [(i, i ^ stride) for i in range(size)])]
    ppermute x32, waiting for transfers between devices: 45.3 us -> 25.3 us  [shifted(): return lax.ppermute(block, axis, route)]
    ppermute x32, starting transfers between devices: 25 us -> 44.3 us  [shifted(): return lax.ppermute(block, axis, route)]
    all_gather x1, waiting for transfers between devices: 11.9 us -> 0.01 us  [body(): key_piece = lax.all_gather(keys_own, 'seq', axis=1, tiled=True)]
    unnamed x130 -> x128, local copies, waits for them, and re-layouts: 122 us -> 122 us
  transfers between devices with their start and end apart: 35 -> 37, of which waited for: 19 -> 20; matrix products, arithmetic and copies ran while one was open for 11% -> 12% of each run, Pallas kernels for 0% -> 0%
where the time goes in v1:
time: 1160 us; the launch traced here: 1150 us
  blocking collectives  519 us (45%)
  local copies, waits for them, and re-layouts  279 us (24%)
  other arithmetic  112 us (10%)
  matrix products  86.9 us (7%)
  waiting for transfers between devices  83 us (7%)
  starting transfers between devices  51.6 us (4%)
  between operations  14.9 us (1%)
    unnamed x1, blocking collectives  491 us
    unnamed x128, local copies, waits for them, and re-layouts  122 us
    ppermute x32, starting transfers between devices, shifted(): return lax.ppermute(block, axis, route)  44.3 us
    convert_element_type x1, other arithmetic, body(): lax.all_gather(shares.astype(jnp.bfloat16), 'rows', axis=0, tiled=True)  43.7 us
    reshape x1, local copies, waits for them, and re-layouts, body(): flat_grads.reshape(seq_count * row_count_axis, (share_width + padding) //...  41 us
    reshape x8, local copies, waits for them, and re-layouts, body(): laid_out.append(grad_piece.reshape(seq_count, -1))  30.7 us
    all_gather x1, waiting for transfers between devices, body(): lax.all_gather(shares.astype(jnp.bfloat16), 'rows', axis=0, tiled=True)  30.6 us
    all_gather x1, blocking collectives, body(): all_docs = lax.all_gather(segment_ids, 'seq', axis=1, tiled=True)  28.4 us
  transfers between devices with their start and end apart: 37, of which 20 were waited for; matrix products, arithmetic and copies ran while one was open for 12% of the time, Pallas kernels for 0%

profile of v1, /device:TPU:0, one launch (start us, length us, event | category | flops | bytes accessed | tf_op | source)
XLA Modules:
  0.0 1147.2 jit_solution(12963509451318854085)
XLA Ops:
  15.6 3.0 collective-permute-start.4
  18.6 5.2 collective-permute-done.4
  27.6 14.5 %collective-permute-done.5 = bf16[2,1,128,768]{3,2,0,1:T(8,128)(2,1)} collective-permute-done((bf16[2,1,128,768]{3,2,0,1:T(8,128)(2,1)}, bf16[2,1,128,768]{3,2,0,1:T(8,128)(2,1)}, u32[]{:S(2)}, u32[]{:S(2)}) %collective-permute-start.5) | collective-permute-done | bytes 393248 | tf_op jit(solution)/shard_map/ppermute | solution.py:27
  44.3 2.4 collective-permute-start.6
  55.3 28.4 %all_gather.11 = s32[1,1024]{1,0:T(1,128)S(1)} all-gather(s32[1,128]{1,0:T(1,128)S(1)} %copy-done.36), channel_id=1, replica_groups=mesh['seq'=8,'rows'=4] {'seq'}, dimensions={1}, use_global_device_ids=true | all-gather | bytes 4608 | tf_op jit(solution)/shard_map/all_gather | solution.py:89
  85.8 7.4 collective-permute-done.6
  96.2 3.8 copy.45
  100.0 3.8 reshape.640
  103.8 2.6 copy.44
  106.4 2.7 select_reduce_fusion
  109.1 2.0 fusion.15
  111.8 2.4 fusion.85
  115.0 4.2 multiply_convert_fusion
  122.8 2.5 convert_reduce_fusion.1
  125.3 2.4 multiply_reduce_fusion
  134.1 193.1 %while.30 = (s32[]{:T(128)}, bf16[1,128,768]{1,2,0:T(8,128)(2,1)}, bf16[1,128,768]{1,2,0:T(8,128)(2,1)}, f32[1,128,768]{1,2,0:T(8,128)}, f32[1,128,768]{1,2,0:T(...) while((s32[]{:T(128)}, bf16[1,128,768]{1,2,0:T(8,128)(2,1)}, ...), condition=%wide.region_11.12_spmd.clone, body=%wide.region_10.11_spmd.clone.sunk | while | flops 128401424 | bytes 19905180 | solution.py:245
  136.0 9.9 collective-permute-start
  147.5 3.1 collective-permute-start.1
  160.0 2.2 fusion.151
  162.2 2.6 collective-permute-done.2
  181.6 2.3 fusion.151
  183.9 3.6 collective-permute-done.2
  201.1 3.6 collective-permute-start.3
  204.7 2.3 fusion.151
  207.0 3.1 collective-permute-done.2
  228.0 2.3 fusion.151
  230.3 2.7 collective-permute-done.2
  248.6 2.1 collective-permute-start.3
  250.6 2.3 fusion.151
  253.0 2.7 collective-permute-done.2
  271.2 2.0 collective-permute-start.3
  273.2 2.3 fusion.151
  275.6 2.6 collective-permute-done.2
  294.2 2.0 collective-permute-start.3
  296.1 2.3 fusion.151
  298.5 2.4 collective-permute-done.2
  316.8 2.0 collective-permute-start.3
  318.8 2.3 fusion.151
  321.1 2.3 collective-permute-done.2
  331.3 2.1 convolution_add_fusion.2
  333.4 4.0 fusion.49
  339.3 5.0 fusion.74
  344.4 5.0 fusion.89
  349.4 7.1 reshape.648
  356.5 5.5 constant_dynamic-update-slice_fusion.1
  362.2 2.1 reshape.649
  364.3 8.9 reshape.651
  373.3 8.9 reshape.653
  383.2 2.6 fusion.59
  385.7 3.5 reshape.657
  390.6 7.5 dynamic-update-slice.2
  399.5 26.5 %dynamic-update-slice.4 = f32[8,959616]{1,0:T(8,128)} dynamic-update-slice(f32[8,959616]{1,0:T(8,128)} %dynamic-update-slice.3, f32[8,294912]{1,0:T(8,128)} %reshape.651, s32[]{} %constant.214, s32[]{} %constant.219) | dynamic-update-slice | bytes 18874372
  427.5 26.6 %dynamic-update-slice.6 = f32[8,959616]{1,0:T(8,128)} dynamic-update-slice(f32[8,959616]{1,0:T(8,128)} %dynamic-update-slice.5, f32[8,294912]{1,0:T(8,128)} %reshape.653, s32[]{} %constant.214, s32[]{} %constant.221) | dynamic-update-slice | bytes 18874372
  460.0 37.1 %reshape.687 = f32[7676928]{0:T(1024)} reshape(f32[8,959616]{1,0:T(8,128)} %constant_dynamic-update-slice_fusion) | data formatting | bytes 61415424
  497.2 41.0 %reshape.658 = f32[32,239904]{1,0:T(8,128)} reshape(f32[7676928]{0:T(1024)} %reshape.687) | data formatting | bytes 61415424 | tf_op jit(solution)/shard_map/reshape | solution.py:299
  538.1 490.6 %all-reduce.2 = bf16[32,239904]{1,0:T(8,128)(2,1)} all-reduce(f32[32,239904]{1,0:T(8,128)} %reshape.658), channel_id=3, replica_groups=mesh['seq'=8,'rows'=4] {'seq','rows'}, use_global_device_ids=true, to_apply=%region_21.22.clone | all-reduce | flops 7676928 | bytes 46061568
  1028.7 3.4 fusion.36
  1032.1 30.6 %all-gather.7.cloned.1.call-done = bf16[4,1,239904]{2,1,0:T(2,128)(2,1)} async-done(((bf16[1,1,239904]{2,1,0:T(2,128)(2,1)}), bf16[4,1,239904]{2,1,0:T(2,128)(2,1)}) %all-gather.7.cloned.1.call-update) | async-done | bytes 1919248 | tf_op jit(solution)/shard_map/all_gather | solution.py:303
  1062.7 43.7 %convert_reduce_fusion = f32[4,239904]{1,0:T(4,128)} fusion(bf16[4,1,239904]{2,1,0:T(2,128)(2,1)} %all-gather.7.cloned.1.call-done), kind=kLoop, calls=%fused_computation.27 | loop fusion | flops 959616 | bytes 5757696 | tf_op jit(solution)/shard_map/convert_element_type | solution.py:303
  1106.4 6.5 reshape.659
  1117.3 3.9 fusion.83
  1121.8 8.4 slice.82
  1132.0 2.6 reshape.662
  1134.6 2.4 reshape.663
  (431 shorter events, 193.7 us)
Async XLA Ops:
  7.2 96.6 %all-gather.5.cloned.1.call-start = ((), (), s32[]{:S(2)}) async-start(), calls=%async_computation | async-start | bytes 1769472 | tf_op jit(solution)/shard_map/all_gather | solution.py:109
  13.6 1049.1 %all-gather.7.cloned.1.call-start = ((), (), s32[]{:S(2)}) async-start(), calls=%async_computation.1 | async-start | bytes 4800000 | tf_op jit(solution)/shard_map/all_gather | solution.py:303
  15.6 8.2 collective-permute-start.4
  25.8 16.3 %collective-permute-start.5 = (bf16[2,1,128,768]{3,2,0,1:T(8,128)(2,1)}, bf16[2,1,128,768]{3,2,0,1:T(8,128)(2,1)}, u32[]{:S(2)}, u32[]{:S(2)}) collective-permute-start(bf16[2,1,128,768]{3,2,0,1:T(8,128)(2,1)} %get-tuple-element.498), channel_id=1, source_target_pairs={{0,8},{4,12},{8,0},{12,4},{16,24},{20,28},{24,16},{28,20},{1,9},{5... | collective-permute-start | bytes 1179656 | tf_op jit(solution)/shard_map/ppermute | solution.py:27
  43.3 12.0 %copy-start.36 = (s32[1,128]{1,0:T(1,128)S(1)}, s32[1,128]{1,0:T(1,128)}, u32[]{:S(2)}) copy-start(s32[1,128]{1,0:T(1,128)} %param.19) | copy-start | bytes 1540
  44.3 48.9 %collective-permute-start.6 = (bf16[4,1,128,768]{3,2,0,1:T(8,128)(2,1)}, bf16[4,1,128,768]{3,2,0,1:T(8,128)(2,1)}, u32[]{:S(2)}, u32[]{:S(2)}) collective-permute-start(bf16[4,1,128,768]{3,2,0,1:T(8,128)(2,1)} %bitcast.15), channel_id=1, source_target_pairs={{0,16},{4,20},{8,24},{12,28},{16,0},{20,4},{24,8},{28,12},{1,17},{... | collective-permute-start | bytes 2359304 | tf_op jit(solution)/shard_map/ppermute | solution.py:27
  83.6 9.6 copy-start.45
  114.2 5.0 copy-start.27
  114.2 5.0 slice-start.1
  114.7 13.0 %copy-start.4 = (f32[128,768]{1,0:T(8,128)}, f32[128,768]{1,0:T(8,128)S(1)}, u32[]{:S(2)}) copy-start(f32[128,768]{1,0:T(8,128)S(1)} %get-tuple-element.510) | copy-start | bytes 1179652
  114.7 13.0 %copy-start.38 = (f32[128]{0:T(128)}, f32[128]{0:T(128)S(1)}, u32[]{:S(2)}) copy-start(f32[128]{0:T(128)S(1)} %broadcast_multiply_fusion.1) | copy-start | bytes 1540
  114.9 12.8 %copy-start.49 = (f32[128]{0:T(128)}, f32[128]{0:T(128)S(1)}, u32[]{:S(2)}) copy-start(f32[128]{0:T(128)S(1)} %fusion.65) | copy-start | bytes 1540
  136.0 32.8 %collective-permute-start = (bf16[1,128,768]{1,2,0:T(8,128)(2,1)}, bf16[1,128,768]{1,2,0:T(8,128)(2,1)}, u32[]{:S(2)}, u32[]{:S(2)}) collective-permute-start(bf16[1,128,768]{1,2,0:T(8,128)(2,1)} %copy.66), channel_id=1, source_target_pairs={{28,0},{0,4},{4,8},{8,12},{12,16},{16,20},{20,24},{24,28},{29,1},{... | collective-permute-start | bytes 589832 | tf_op jit(solution)/shard_map/while/body/eval_jaxpr/ppermute | solution.py:37
  147.5 21.3 %collective-permute-start.1 = (bf16[1,128,768]{1,2,0:T(8,128)(2,1)}, bf16[1,128,768]{1,2,0:T(8,128)(2,1)}, u32[]{:S(2)}, u32[]{:S(2)}) collective-permute-start(bf16[1,128,768]{1,2,0:T(8,128)(2,1)} %copy.67), channel_id=1, source_target_pairs={{28,0},{0,4},{4,8},{8,12},{12,16},{16,20},{20,24},{24,28},{29,1},{... | collective-permute-start | bytes 589832 | tf_op jit(solution)/shard_map/while/body/eval_jaxpr/ppermute | solution.py:37
  150.7 4.4 copy-start.9
  156.1 8.7 collective-permute-start.2
  158.4 8.7 collective-permute-start.3
  170.4 21.0 %collective-permute-start = (bf16[1,128,768]{1,2,0:T(8,128)(2,1)}, bf16[1,128,768]{1,2,0:T(8,128)(2,1)}, u32[]{:S(2)}, u32[]{:S(2)}) collective-permute-start(bf16[1,128,768]{1,2,0:T(8,128)(2,1)} %copy.66), channel_id=1, source_target_pairs={{28,0},{0,4},{4,8},{8,12},{12,16},{16,20},{20,24},{24,28},{29,1},{... | collective-permute-start | bytes 589832 | tf_op jit(solution)/shard_map/while/body/eval_jaxpr/ppermute | solution.py:37
  172.0 19.3 %collective-permute-start.1 = (bf16[1,128,768]{1,2,0:T(8,128)(2,1)}, bf16[1,128,768]{1,2,0:T(8,128)(2,1)}, u32[]{:S(2)}, u32[]{:S(2)}) collective-permute-start(bf16[1,128,768]{1,2,0:T(8,128)(2,1)} %copy.67), channel_id=1, source_target_pairs={{28,0},{0,4},{4,8},{8,12},{12,16},{16,20},{20,24},{24,28},{29,1},{... | collective-permute-start | bytes 589832 | tf_op jit(solution)/shard_map/while/body/eval_jaxpr/ppermute | solution.py:37
  178.6 8.9 collective-permute-start.2
  179.9 9.7 collective-permute-start.3
  193.0 21.0 %collective-permute-start = (bf16[1,128,768]{1,2,0:T(8,128)(2,1)}, bf16[1,128,768]{1,2,0:T(8,128)(2,1)}, u32[]{:S(2)}, u32[]{:S(2)}) collective-permute-start(bf16[1,128,768]{1,2,0:T(8,128)(2,1)} %copy.66), channel_id=1, source_target_pairs={{28,0},{0,4},{4,8},{8,12},{12,16},{16,20},{20,24},{24,28},{29,1},{... | collective-permute-start | bytes 589832 | tf_op jit(solution)/shard_map/while/body/eval_jaxpr/ppermute | solution.py:37
  194.6 19.3 %collective-permute-start.1 = (bf16[1,128,768]{1,2,0:T(8,128)(2,1)}, bf16[1,128,768]{1,2,0:T(8,128)(2,1)}, u32[]{:S(2)}, u32[]{:S(2)}) collective-permute-start(bf16[1,128,768]{1,2,0:T(8,128)(2,1)} %copy.67), channel_id=1, source_target_pairs={{28,0},{0,4},{4,8},{8,12},{12,16},{16,20},{20,24},{24,28},{29,1},{... | collective-permute-start | bytes 589832 | tf_op jit(solution)/shard_map/while/body/eval_jaxpr/ppermute | solution.py:37
  194.6 4.4 copy-start.9
  200.1 10.0 collective-permute-start.2
  201.1 11.1 collective-permute-start.3
  215.5 21.3 %collective-permute-start = (bf16[1,128,768]{1,2,0:T(8,128)(2,1)}, bf16[1,128,768]{1,2,0:T(8,128)(2,1)}, u32[]{:S(2)}, u32[]{:S(2)}) collective-permute-start(bf16[1,128,768]{1,2,0:T(8,128)(2,1)} %copy.66), channel_id=1, source_target_pairs={{28,0},{0,4},{4,8},{8,12},{12,16},{16,20},{20,24},{24,28},{29,1},{... | collective-permute-start | bytes 589832 | tf_op jit(solution)/shard_map/while/body/eval_jaxpr/ppermute | solution.py:37
  217.2 19.7 %collective-permute-start.1 = (bf16[1,128,768]{1,2,0:T(8,128)(2,1)}, bf16[1,128,768]{1,2,0:T(8,128)(2,1)}, u32[]{:S(2)}, u32[]{:S(2)}) collective-permute-start(bf16[1,128,768]{1,2,0:T(8,128)(2,1)} %copy.67), channel_id=1, source_target_pairs={{28,0},{0,4},{4,8},{8,12},{12,16},{16,20},{20,24},{24,28},{29,1},{... | collective-permute-start | bytes 589832 | tf_op jit(solution)/shard_map/while/body/eval_jaxpr/ppermute | solution.py:37
  223.9 9.2 collective-permute-start.2
  226.2 9.0 collective-permute-start.3
  238.5 21.0 %collective-permute-start = (bf16[1,128,768]{1,2,0:T(8,128)(2,1)}, bf16[1,128,768]{1,2,0:T(8,128)(2,1)}, u32[]{:S(2)}, u32[]{:S(2)}) collective-permute-start(bf16[1,128,768]{1,2,0:T(8,128)(2,1)} %copy.66), channel_id=1, source_target_pairs={{28,0},{0,4},{4,8},{8,12},{12,16},{16,20},{20,24},{24,28},{29,1},{... | collective-permute-start | bytes 589832 | tf_op jit(solution)/shard_map/while/body/eval_jaxpr/ppermute | solution.py:37
  240.2 19.3 %collective-permute-start.1 = (bf16[1,128,768]{1,2,0:T(8,128)(2,1)}, bf16[1,128,768]{1,2,0:T(8,128)(2,1)}, u32[]{:S(2)}, u32[]{:S(2)}) collective-permute-start(bf16[1,128,768]{1,2,0:T(8,128)(2,1)} %copy.67), channel_id=1, source_target_pairs={{28,0},{0,4},{4,8},{8,12},{12,16},{16,20},{20,24},{24,28},{29,1},{... | collective-permute-start | bytes 589832 | tf_op jit(solution)/shard_map/while/body/eval_jaxpr/ppermute | solution.py:37
  246.5 9.1 collective-permute-start.2
  248.6 9.2 collective-permute-start.3
  261.1 21.0 %collective-permute-start = (bf16[1,128,768]{1,2,0:T(8,128)(2,1)}, bf16[1,128,768]{1,2,0:T(8,128)(2,1)}, u32[]{:S(2)}, u32[]{:S(2)}) collective-permute-start(bf16[1,128,768]{1,2,0:T(8,128)(2,1)} %copy.66), channel_id=1, source_target_pairs={{28,0},{0,4},{4,8},{8,12},{12,16},{16,20},{20,24},{24,28},{29,1},{... | collective-permute-start | bytes 589832 | tf_op jit(solution)/shard_map/while/body/eval_jaxpr/ppermute | solution.py:37
  262.7 19.3 %collective-permute-start.1 = (bf16[1,128,768]{1,2,0:T(8,128)(2,1)}, bf16[1,128,768]{1,2,0:T(8,128)(2,1)}, u32[]{:S(2)}, u32[]{:S(2)}) collective-permute-start(bf16[1,128,768]{1,2,0:T(8,128)(2,1)} %copy.67), channel_id=1, source_target_pairs={{28,0},{0,4},{4,8},{8,12},{12,16},{16,20},{20,24},{24,28},{29,1},{... | collective-permute-start | bytes 589832 | tf_op jit(solution)/shard_map/while/body/eval_jaxpr/ppermute | solution.py:37
  263.7 4.4 copy-start.9
  269.1 9.1 collective-permute-start.2
  271.2 9.1 collective-permute-start.3
  283.7 21.0 %collective-permute-start = (bf16[1,128,768]{1,2,0:T(8,128)(2,1)}, bf16[1,128,768]{1,2,0:T(8,128)(2,1)}, u32[]{:S(2)}, u32[]{:S(2)}) collective-permute-start(bf16[1,128,768]{1,2,0:T(8,128)(2,1)} %copy.66), channel_id=1, source_target_pairs={{28,0},{0,4},{4,8},{8,12},{12,16},{16,20},{20,24},{24,28},{29,1},{... | collective-permute-start | bytes 589832 | tf_op jit(solution)/shard_map/while/body/eval_jaxpr/ppermute | solution.py:37
  285.3 19.4 %collective-permute-start.1 = (bf16[1,128,768]{1,2,0:T(8,128)(2,1)}, bf16[1,128,768]{1,2,0:T(8,128)(2,1)}, u32[]{:S(2)}, u32[]{:S(2)}) collective-permute-start(bf16[1,128,768]{1,2,0:T(8,128)(2,1)} %copy.67), channel_id=1, source_target_pairs={{28,0},{0,4},{4,8},{8,12},{12,16},{16,20},{20,24},{24,28},{29,1},{... | collective-permute-start | bytes 589832 | tf_op jit(solution)/shard_map/while/body/eval_jaxpr/ppermute | solution.py:37
  286.7 4.4 copy-start.9
  292.1 8.7 collective-permute-start.2
  294.2 8.8 collective-permute-start.3
  306.3 21.0 %collective-permute-start = (bf16[1,128,768]{1,2,0:T(8,128)(2,1)}, bf16[1,128,768]{1,2,0:T(8,128)(2,1)}, u32[]{:S(2)}, u32[]{:S(2)}) collective-permute-start(bf16[1,128,768]{1,2,0:T(8,128)(2,1)} %copy.66), channel_id=1, source_target_pairs={{28,0},{0,4},{4,8},{8,12},{12,16},{16,20},{20,24},{24,28},{29,1},{... | collective-permute-start | bytes 589832 | tf_op jit(solution)/shard_map/while/body/eval_jaxpr/ppermute | solution.py:37
  307.9 19.3 %collective-permute-start.1 = (bf16[1,128,768]{1,2,0:T(8,128)(2,1)}, bf16[1,128,768]{1,2,0:T(8,128)(2,1)}, u32[]{:S(2)}, u32[]{:S(2)}) collective-permute-start(bf16[1,128,768]{1,2,0:T(8,128)(2,1)} %copy.67), channel_id=1, source_target_pairs={{28,0},{0,4},{4,8},{8,12},{12,16},{16,20},{20,24},{24,28},{29,1},{... | collective-permute-start | bytes 589832 | tf_op jit(solution)/shard_map/while/body/eval_jaxpr/ppermute | solution.py:37
  314.6 8.8 collective-permute-start.2
  316.8 8.7 collective-permute-start.3
  339.3 5.1 copy-start.17
  339.3 5.1 copy-start.30
  356.5 5.5 copy-start.44
  364.3 8.9 copy-start.51
  373.3 9.0 copy-start.42
  373.3 9.1 copy-start.41
  373.3 9.2 copy-start.48
  373.3 9.3 copy-start.47
  373.3 9.4 copy-start.46
  373.3 9.5 copy-start.31
  373.3 9.5 copy-start.37
  373.3 9.8 copy-start.33
  373.3 9.8 copy-start.35
  427.5 31.0 %copy-start.10 = (f32[8,73728]{1,0:T(8,128)S(1)}, f32[8,73728]{1,0:T(8,128)}, u32[]{:S(2)}) copy-start(f32[8,73728]{1,0:T(8,128)} %reshape.657) | copy-start | bytes 7077892
  1121.8 8.4 slice-start
  1132.0 8.1 copy-start.1
  (71 other events, 177.5 us)
Sparse Core Ops, SparseCore 0:
  13.8 69.2 all-gather.4
  1032.2 30.4 all-gather.6
